TPU v7x, 256 devices: a whole 4x4x8 slice. The times are simulated.
256 devices in a mesh: fib: 8 (over y, x_hi), rest: 32 (over z, x_lo, core).
Axes of the slice: x: 4 (x_hi: 2, x_lo: 2; x = x_hi * 2 + x_lo), y: 4, z: 8, core: 2. Of those that a mesh axis runs over, the one named last changes fastest.
Arguments:
- tensor: float32 [64, 128, 64, 1024], P('fib', 'rest'), may hold values from -24 to 24
- factor_one: float32 [1024, 128], replicated, may hold values from 0 to 0.05
- factor_two: float32 [64, 128], P('fib'), may hold values from 0.05 to 0.35
- factor_three: float32 [128, 128], P('rest'), may hold values from 0.03 to 0.25
- factor_four: float32 [64, 128], replicated, may hold values from 0.03 to 0.25
Outputs:
- new_factor: float32 [1024, 128], replicated
- factor_gram: float32 [128, 128], replicated
All inputs are finite; a program needn't handle non-finite values.
Results may differ from a plain program's by a relative error of at most 0.00014.
Values sent between devices are 32-bit elements; how exact they have to be, the bound alone decides.
No kernel may reach another device: no remote copies, remote signals or barrier semaphores. Data moves between devices by JAX's collectives and lax.ppermute only.
A program may use at most 64 MiB of HBM per device.

v0:
```python
import jax
import jax.numpy as jnp
from jax import lax
from jax.sharding import PartitionSpec as P


def from_everyone(value, axis):
    size = lax.axis_size(axis)
    return lax.all_to_all(
        jnp.broadcast_to(value[None], (size, *value.shape)), axis, 0, 0, tiled=True
    )


def of_everyone(value, axis):
    everything = from_everyone(value, axis)
    return jnp.sum(everything, axis=0)


def gathered_total(value, axis):
    return lax.all_gather(value, axis).sum(0)


def hals_columns(factor, mttkrp, gram_v):
    highest = lax.Precision.HIGHEST
    rank_cols = factor.shape[1]
    width = 16
    current = factor
    for block_idx in range(rank_cols // width):
        lower = block_idx * width
        base = jnp.dot(current, gram_v[:, lower : lower + width], precision=highest)
        old_cols = current[:, lower : lower + width]
        inner = gram_v[lower : lower + width, lower : lower + width]
        target = mttkrp[:, lower : lower + width]

        def update(k, cols):
            index = k.astype(jnp.int32)
            zero = jnp.zeros((), jnp.int32)
            inner_col = lax.dynamic_slice_in_dim(inner, index, 1, 1)
            diag = lax.dynamic_slice_in_dim(inner_col, index, 1, 0)[0, 0]
            product = (
                lax.dynamic_slice_in_dim(base, index, 1, 1)[:, 0]
                + jnp.dot(cols - old_cols, inner_col, precision=highest)[:, 0]
            )
            goal = lax.dynamic_slice_in_dim(target, index, 1, 1)[:, 0]
            column = lax.dynamic_slice_in_dim(cols, index, 1, 1)[:, 0]
            fresh = jnp.maximum(column + (goal - product) / diag, 0.0)
            return lax.dynamic_update_slice(cols, fresh[:, None], (zero, index))

        cols = lax.fori_loop(0, width, update, old_cols)
        current = current.at[:, lower : lower + width].set(cols)
    return current


def per_device(tensor, factor_one, factor_two, factor_three, factor_four):
    highest = lax.Precision.HIGHEST
    rank_cols = factor_one.shape[1]
    mode_one = tensor.shape[3]
    khatri = (
        factor_two[:, None, None, :]
        * factor_three[None, :, None, :]
        * factor_four[None, None, :, :]
    ).reshape(-1, rank_cols)
    flat = tensor.reshape(-1, mode_one)
    part_two = jnp.dot(factor_two.T, factor_two, precision=highest)
    part_three = jnp.dot(factor_three.T, factor_three, precision=highest)
    gram_four = jnp.dot(factor_four.T, factor_four, precision=highest)
    gram_two = of_everyone(part_two, "fib")
    gram_three = gathered_total(part_three, "rest")
    gram_v = gram_two * gram_three * gram_four
    partial_value = lax.dot_general(flat, khatri, (((0,), (0,)), ((), ())), precision=highest)
    mttkrp = lax.psum(partial_value, ("fib", "rest"))
    new_factor = hals_columns(factor_one, mttkrp, gram_v)
    factor_gram = jnp.dot(new_factor.T, new_factor, precision=highest)
    return (new_factor, factor_gram)


def solution(mesh):
    return jax.shard_map(
        per_device,
        mesh=mesh,
        in_specs=(P("fib", "rest", None, None), P(), P("fib", None), P("rest", None), P()),
        out_specs=(P(), P()),
        check_vma=False,
    )
```

profile of v0, /device:TPU:1, one launch (start us, length us, event | category | flops | bytes accessed | tf_op | source)
XLA Modules:
  0.0 526.1 jit_solution(3609673047529688155)
XLA Ops:
  8.1 1.0 copy.149
  9.8 7.8 %convolution_bitcast_fusion.8 = f32[1024,128]{0,1:T(8,128)} fusion(f32[8,4,64,1024]{3,2,1,0:T(8,128)} %param.37, f32[64,128]{1,0:T(8,128)} %param.41, f32[8,4,128]{2,1,0:T(4,128)S(1)} %broadcast_multiply_fusion), kind=kOutput, calls=%fused_computation.64 | convolution fusion | flops 3221487616 | bytes 8962048 | tf_op jit(solution)/shard_map/dot_general | solution.py:70
  17.8 0.9 fusion.69
  19.9 7.5 %all-to-all-start = ((f32[8,128,128]{2,1,0:T(8,128)}), f32[8,128,128]{2,1,0:T(8,128)S(1)}, u32[]{:S(2)}, u32[]{:S(2)}) async-start(f32[8,128,128]{2,1,0:T(8,128)} %broadcast_in_dim.33), calls=%async_computation | async-start | bytes 1048576 | tf_op jit(solution)/shard_map/all_to_all | solution.py:9
  32.2 244.8 %all-reduce.2.cloned.1.call-done = f32[1024,128]{0,1:T(8,128)} async-done(((f32[1024,128]{0,1:T(8,128)}), f32[1024,128]{0,1:T(8,128)}) %all-reduce.2.cloned.1.call-update) | async-done | bytes 524304 | tf_op jit(solution)/shard_map/psum | solution.py:71
  277.0 1.1 fusion.66
  278.3 1.7 reduce_sum.19
  281.0 24.8 %while.136 = (s32[]{:T(128)}, f32[1024,16]{0,1:T(8,128)S(1)}, f32[1024,16]{0,1:T(8,128)S(1)}, f32[1024,16]{0,1:T(8,128)S(1)}, f32[1024,16]{0,1:T(8,128)S(1)}, /*...) while((s32[]{:T(128)}, f32[1024,16]{0,1:T(8,128)S(1)}, f32[1024,16]{0,1:T(8,128)S(1)}, ...), condition=%wide.region_5.0_spmd, body=%wide.region_4.0_spmd.sunk | while | flops 218115 | bytes 157821 | solution.py:49
  306.7 2.3 scatter.26
  309.9 24.7 %while.137 = (s32[]{:T(128)}, f32[1024,16]{0,1:T(8,128)S(1)}, f32[1024,16]{0,1:T(8,128)S(1)}, f32[1024,16]{0,1:T(8,128)S(1)}, f32[1024,16]{0,1:T(8,128)S(1)}, /*...) while((s32[]{:T(128)}, f32[1024,16]{0,1:T(8,128)S(1)}, f32[1024,16]{0,1:T(8,128)S(1)}, ...), condition=%wide.region_8.0_spmd, body=%wide.region_7.0_spmd.sunk | while | flops 218115 | bytes 157821 | solution.py:49
  335.7 3.1 scatter.29
  339.7 24.8 %while.138 = (s32[]{:T(128)}, f32[1024,16]{0,1:T(8,128)S(1)}, f32[1024,16]{0,1:T(8,128)S(1)}, f32[1024,16]{0,1:T(8,128)S(1)}, f32[1024,16]{0,1:T(8,128)S(1)}, /*...) while((s32[]{:T(128)}, f32[1024,16]{0,1:T(8,128)S(1)}, f32[1024,16]{0,1:T(8,128)S(1)}, ...), condition=%wide.region_11.0_spmd, body=%wide.region_10.0_spmd.sunk | while | flops 218115 | bytes 157821 | solution.py:49
  365.5 3.1 scatter.30
  369.6 24.7 %while.139 = (s32[]{:T(128)}, f32[1024,16]{0,1:T(8,128)S(1)}, f32[1024,16]{0,1:T(8,128)S(1)}, f32[1024,16]{0,1:T(8,128)S(1)}, f32[1024,16]{0,1:T(8,128)S(1)}, /*...) while((s32[]{:T(128)}, f32[1024,16]{0,1:T(8,128)S(1)}, f32[1024,16]{0,1:T(8,128)S(1)}, ...), condition=%wide.region_14.0_spmd, body=%wide.region_13.0_spmd.sunk | while | flops 218115 | bytes 157821 | solution.py:49
  395.3 3.1 scatter.31
  399.3 24.8 %while.140 = (s32[]{:T(128)}, f32[1024,16]{0,1:T(8,128)S(1)}, f32[1024,16]{0,1:T(8,128)S(1)}, f32[1024,16]{0,1:T(8,128)S(1)}, f32[1024,16]{0,1:T(8,128)S(1)}, /*...) while((s32[]{:T(128)}, f32[1024,16]{0,1:T(8,128)S(1)}, f32[1024,16]{0,1:T(8,128)S(1)}, ...), condition=%wide.region_17.0_spmd, body=%wide.region_16.0_spmd.sunk | while | flops 218115 | bytes 157821 | solution.py:49
  425.1 3.1 scatter.34
  429.1 24.7 %while.141 = (s32[]{:T(128)}, f32[1024,16]{0,1:T(8,128)S(1)}, f32[1024,16]{0,1:T(8,128)S(1)}, f32[1024,16]{0,1:T(8,128)S(1)}, f32[1024,16]{0,1:T(8,128)S(1)}, /*...) while((s32[]{:T(128)}, f32[1024,16]{0,1:T(8,128)S(1)}, f32[1024,16]{0,1:T(8,128)S(1)}, ...), condition=%wide.region_20.0_spmd, body=%wide.region_19.0_spmd.sunk | while | flops 218115 | bytes 157821 | solution.py:49
  454.8 3.1 scatter.35
  458.8 24.7 %while.142 = (s32[]{:T(128)}, f32[1024,16]{0,1:T(8,128)S(1)}, f32[1024,16]{0,1:T(8,128)S(1)}, f32[1024,16]{0,1:T(8,128)S(1)}, f32[1024,16]{0,1:T(8,128)S(1)}, /*...) while((s32[]{:T(128)}, f32[1024,16]{0,1:T(8,128)S(1)}, f32[1024,16]{0,1:T(8,128)S(1)}, ...), condition=%wide.region_23.0_spmd, body=%wide.region_22.0_spmd.sunk | while | flops 218115 | bytes 157821 | solution.py:49
  484.7 3.3 scatter.36
  488.9 24.8 %while.143 = (s32[]{:T(128)}, f32[1024,16]{0,1:T(8,128)S(1)}, f32[1024,16]{0,1:T(8,128)S(1)}, f32[1024,16]{0,1:T(8,128)S(1)}, f32[1024,16]{0,1:T(8,128)S(1)}, /*...) while((s32[]{:T(128)}, f32[1024,16]{0,1:T(8,128)S(1)}, f32[1024,16]{0,1:T(8,128)S(1)}, ...), condition=%wide.region_25.0_spmd, body=%wide.region_24.0_spmd.sunk | while | flops 218115 | bytes 157821 | solution.py:49
  513.9 3.1 scatter.39
  517.0 1.6 fusion.70
  (459 shorter events, 215.6 us)
Async XLA Ops:
  8.0 10.7 %copy-start.2 = (f32[8,128]{1,0:T(8,128)S(1)}, f32[8,128]{1,0:T(8,128)}, u32[]{:S(2)}) copy-start(f32[8,128]{1,0:T(8,128)} %param.39) | copy-start | bytes 12292
  8.0 9.7 %copy-start.3 = (f32[4,128]{1,0:T(4,128)S(1)}, f32[4,128]{1,0:T(4,128)}, u32[]{:S(2)}) copy-start(f32[4,128]{1,0:T(4,128)} %param.40) | copy-start | bytes 6148
  8.0 272.1 %copy-start.1 = (f32[64,128]{1,0:T(8,128)S(1)}, f32[64,128]{1,0:T(8,128)}, u32[]{:S(2)}) copy-start(f32[64,128]{1,0:T(8,128)} %param.41) | copy-start | bytes 98308
  8.0 269.0 %all-reduce.2.cloned.1.call-start = ((), (), s32[]{:S(2)}) async-start(), calls=%async_computation.1 | async-start | bytes 1048576 | tf_op jit(solution)/shard_map/psum | solution.py:71
  17.7 260.6 %all-gather.3.cloned.1.call-start = ((), (), s32[]{:S(2)}) async-start(), calls=%async_computation.2 | async-start | bytes 2162688 | tf_op jit(solution)/shard_map/all_gather | solution.py:20
  19.9 258.3 %all-to-all-start = ((f32[8,128,128]{2,1,0:T(8,128)}), f32[8,128,128]{2,1,0:T(8,128)S(1)}, u32[]{:S(2)}, u32[]{:S(2)}) async-start(f32[8,128,128]{2,1,0:T(8,128)} %broadcast_in_dim.33), calls=%async_computation | async-start | bytes 1048576 | tf_op jit(solution)/shard_map/all_to_all | solution.py:9
  517.0 1.7 copy-start
Sparse Core Ops, SparseCore 0:
  17.8 259.1 all-reduce.1
Sparse Core Ops, SparseCore 1:
  20.6 68.5 all-gather.2
where the time goes:
time: 528 us; the launch traced here: 526 us
  waiting for transfers between devices  245 us (46%)
  local copies, waits for them, and re-layouts  121 us (23%)
  matrix products  120 us (23%)
  between operations  15.8 us (3%)
  other arithmetic  12.8 us (2%)
  starting transfers between devices  7.55 us (1%)
    psum x1, waiting for transfers between devices, per_device(): mttkrp = lax.psum(partial_value, ('fib', 'rest'))  245 us
    dot_general x128, matrix products, update(): jnp.dot(cols - old_cols, inner_col, precision=highest)[:, 0]  104 us
    dynamic_slice x128, local copies, waits for them, and re-layouts, update(): diag = lax.dynamic_slice_in_dim(inner_col, index, 1, 0)[0, 0]  75.3 us
    scatter x8, local copies, waits for them, and re-layouts, hals_columns(): current = current.at[:, lower:lower + width].set(cols)  23.9 us
    dynamic_update_slice x128, local copies, waits for them, and re-layouts, update(): return lax.dynamic_update_slice(cols, fresh[:, None], (zero, index))  14.1 us
  transfers between devices with their start and end apart: 3, of which 1 were waited for; matrix products, arithmetic and copies ran while one was open for 2% of the time, Pallas kernels for 0%

commit v1 on v0

v1 whole, which is shorter than its diff:
```python
import jax
import jax.numpy as jnp
from jax import lax
from jax.experimental import pallas as pl
from jax.sharding import Mesh, PartitionSpec as P

HIGHEST = lax.Precision.HIGHEST
PLANE = ("y", "xh", "xl")


def transposed_dot(a, b):
    return lax.dot_general(
        a, b, (((0,), (0,)), ((), ())), precision=HIGHEST, preferred_element_type=jnp.float32
    )


def hals_kernel(parts_ref, two_ref, four_ref, old_ref, out_ref):
    rank = old_ref.shape[1]
    rows = old_ref.shape[0]
    mttkrp = parts_ref[0, :rows, :]
    for z in range(1, parts_ref.shape[0]):
        mttkrp = mttkrp + parts_ref[z, :rows, :]
    three = parts_ref[:, rows:, :].reshape(-1, rank)
    two = two_ref[...]
    four = four_ref[...]
    gram = transposed_dot(two, two) * transposed_dot(three, three) * transposed_dot(four, four)
    row = lax.broadcasted_iota(jnp.int32, (rank, rank), 0)
    col = lax.broadcasted_iota(jnp.int32, (rank, rank), 1)
    diag = jnp.where(row == col, gram, 0.0)
    scale_lane = 1.0 / jnp.sum(diag, axis=0, keepdims=True)
    scale_sub = 1.0 / jnp.sum(diag, axis=1, keepdims=True)
    later = jnp.where(row > col, gram, 0.0)
    rest = (
        mttkrp
        - jnp.dot(old_ref[...], later, precision=HIGHEST, preferred_element_type=jnp.float32)
    ) * scale_lane
    earlier = later * scale_sub
    flipped = jnp.concatenate([rest, jnp.zeros((rank - rows, rank), jnp.float32)], axis=0).T
    tiles = rank // 8
    cols = [flipped[8 * j : 8 * j + 8, :] for j in range(tiles)]
    coef = [earlier[8 * j : 8 * j + 8, :] for j in range(tiles)]
    for k in range(rank):
        tile, sub = divmod(k, 8)
        fresh = jnp.broadcast_to(jnp.maximum(cols[tile], 0.0)[sub : sub + 1, :], (8, rank))
        for j in range(tile if sub < 7 else tile + 1, tiles):
            cols[j] = cols[j] - jnp.broadcast_to(coef[j][:, k : k + 1], (8, rank)) * fresh
    new = jnp.maximum(jnp.concatenate(cols, axis=0), 0.0).T[:rows, :]
    out_ref[...] = jnp.broadcast_to(new[None], out_ref.shape)


def per_device(tensor, factor_one, factor_two, factor_three, factor_four):
    rank = factor_one.shape[1]
    mode_one = tensor.shape[3]
    cores = lax.axis_size("c")
    plane = lax.axis_size(PLANE)
    depth = lax.axis_size("z")
    half = mode_one // cores
    rows = half // plane
    core = lax.axis_index("c")
    plane_pos = lax.axis_index(PLANE)
    khatri = (
        factor_two[:, None, None, :]
        * factor_three[None, :, None, :]
        * factor_four[None, None, :, :]
    ).reshape(-1, rank)
    flat = tensor.reshape(-1, mode_one)
    partial = lax.dot_general(flat, khatri, (((0,), (0,)), ((), ())), precision=HIGHEST)
    partial = partial.reshape(cores, half, rank)
    swap = [(0, 1), (1, 0)]
    other = lax.ppermute(
        jnp.concatenate([lax.dynamic_index_in_dim(partial, 1 - core, 0, False), factor_three, factor_three], axis=0),
        "c",
        swap,
    )
    mine = lax.dynamic_index_in_dim(partial, core, 0, False) + other[:half]
    pair_three = jnp.concatenate([factor_three, other[half : half + 4]], axis=0)
    xl = lax.axis_index("xl")
    seg = plane_pos // 2
    two_rows = lax.dynamic_slice_in_dim(factor_two, 4 * xl, 4, 0)
    three_row = lax.dynamic_slice_in_dim(pair_three, seg, 1, 0)
    extra = jnp.concatenate([two_rows, three_row, three_row, three_row, three_row], axis=0)
    blocks = jnp.concatenate(
        [mine.reshape(plane, rows, rank), jnp.broadcast_to(extra[None], (plane, 8, rank))], axis=1
    )
    got = lax.all_to_all(blocks, PLANE, 0, 0, tiled=True)
    own = jnp.sum(got[:, :rows], axis=0)
    two = got[:, rows : rows + 4].reshape(-1, rank)
    three = got[:, rows + 4]
    block = jnp.concatenate([own, three], axis=0)
    parts = lax.all_to_all(
        jnp.broadcast_to(block[None], (depth, *block.shape)), "z", 0, 0, tiled=True
    )
    old = lax.dynamic_slice_in_dim(factor_one, core * half + plane_pos * rows, rows, 0)
    spread = pl.pallas_call(
        hals_kernel,
        out_shape=jax.ShapeDtypeStruct((plane, rows, rank), jnp.float32),
        name="hals",
    )(parts, two, factor_four, old)
    mine_new = lax.all_to_all(spread, PLANE, 0, 0, tiled=True).reshape(half, rank)
    other_new = lax.ppermute(mine_new, "c", swap)
    first = jnp.where(core == 0, mine_new, other_new)
    second = jnp.where(core == 0, other_new, mine_new)
    new_factor = jnp.concatenate([first, second], axis=0)
    factor_gram = jnp.dot(new_factor.T, new_factor, precision=HIGHEST)
    return (new_factor, factor_gram)


def solution(mesh):
    fine = Mesh(mesh.devices.reshape(4, 2, 8, 2, 2), ("y", "xh", "z", "xl", "c"))
    fib = ("y", "xh")
    rest = ("z", "xl", "c")
    return jax.shard_map(
        per_device,
        mesh=fine,
        in_specs=(P(fib, rest, None, None), P(), P(fib, None), P(rest, None), P()),
        out_specs=(P(), P()),
        check_vma=False,
    )
```

time: 528 us -> 68.7 us (0.13)
  waiting for transfers between devices: 245 us -> 9.62 us
  local copies, waits for them, and re-layouts: 121 us -> 3.82 us
  matrix products: 120 us -> 9.23 us
  blocking collectives: 0 us -> 24.7 us
  between operations: 15.8 us -> 0.81 us
  other arithmetic: 12.8 us -> 0.97 us
  starting transfers between devices: 7.55 us -> 15.5 us
    psum x1 -> x0, waiting for transfers between devices: 245 us -> none  [per_device(): mttkrp = lax.psum(partial_value, ('fib', 'rest'))]
    dot_general x141 -> x2, matrix products: 120 us -> 9.23 us  [the longest x1 7.56 us: per_device(): lax.dot_general(flat, khatri, (((0,), (0,)), ((), ())), precision=HIGHEST)]
    dynamic_slice x128 -> x6, local copies, waits for them, and re-layouts: 75.3 us -> 1.34 us  [the longest x1 0.6 us: per_device(): lax.dynamic_slice_in_dim(factor_one, core * half + plane_pos * rows, rows...]
    all_to_all x0 -> x2, blocking collectives: none -> 24.7 us  [the longest x1 13.7 us: per_device(): got = lax.all_to_all(blocks, PLANE, 0, 0, tiled=True)]
    scatter x8 -> x0, local copies, waits for them, and re-layouts: 23.9 us -> none  [hals_columns(): current = current.at[:, lower:lower + width].set(cols)]
    dynamic_update_slice x128 -> x0, local copies, waits for them, and re-layouts: 14.1 us -> none  [update(): return lax.dynamic_update_slice(cols, fresh[:, None], (zero, index))]
    another operation x14 -> x0, other arithmetic: 10.4 us -> none
    all_to_all x1, waiting for transfers between devices: 0.01 us -> 7.46 us  [per_device(): lax.all_to_all(jnp.broadcast_to(block[None], (depth, *block.shape)), 'z',...]
  transfers between devices with their start and end apart: 3 -> 3, of which waited for: 1 -> 3; matrix products, arithmetic and copies ran while one was open for 2% -> 2% of each run, Pallas kernels for 0% -> 0%
where the time goes in v1:
time: 68.7 us; the launch traced here: 68.4 us
  blocking collectives  24.7 us (36%)
  starting transfers between devices  15.5 us (23%)
  waiting for transfers between devices  9.62 us (14%)
  matrix products  9.23 us (13%)
  local copies, waits for them, and re-layouts  3.82 us (6%)
  Pallas kernels  3.76 us (5%)
  other arithmetic  0.97 us (1%)
  between operations  0.81 us (1%)
    all_to_all x1, blocking collectives, per_device(): got = lax.all_to_all(blocks, PLANE, 0, 0, tiled=True)  13.7 us
    all_to_all x1, blocking collectives, per_device(): lax.all_to_all(spread, PLANE, 0, 0, tiled=True).reshape(half, rank)  11.1 us
    all_to_all x1, starting transfers between devices, per_device(): lax.all_to_all(jnp.broadcast_to(block[None], (depth, *block.shape)), 'z',...  8.19 us
    dot_general x1, matrix products, per_device(): lax.dot_general(flat, khatri, (((0,), (0,)), ((), ())), precision=HIGHEST)  7.56 us
    all_to_all x1, waiting for transfers between devices, per_device(): lax.all_to_all(jnp.broadcast_to(block[None], (depth, *block.shape)), 'z',...  7.46 us
    ppermute x1, starting transfers between devices, per_device(): other_new = lax.ppermute(mine_new, 'c', swap)  4 us
    pallas_call x1, Pallas kernels, per_device(): pl.pallas_call(hals_kernel, out_shape=jax.ShapeDtypeStruct((plane, rows,...  3.76 us
    ppermute x1, starting transfers between devices, per_device(): lax.ppermute(jnp.concatenate([lax.dynamic_index_in_dim(partial, 1 - core,...  3.29 us
  transfers between devices with their start and end apart: 3, of which 3 were waited for; matrix products, arithmetic and copies ran while one was open for 2% of the time, Pallas kernels for 0%

profile of v1, /device:TPU:1, one launch (start us, length us, event | category | flops | bytes accessed | tf_op | source)
XLA Modules:
  0.0 68.4 jit_solution(18081494760015104327)
XLA Ops:
  0.6 0.0 copy-start
  0.6 0.0 copy-start.4
  0.7 0.0 copy-start.3
  0.7 0.8 %broadcast_multiply_fusion = f32[8,4,128]{2,1,0:T(4,128)S(1)} fusion(f32[4,128]{1,0:T(4,128)} %param.8, f32[8,128]{1,0:T(8,128)} %param.7), kind=kLoop, calls=%fused_computation.12 | loop fusion | flops 4096 | bytes 22528 | tf_op jit(solution)/shard_map/mul | solution.py:62
  1.4 7.6 %convolution_bitcast_fusion = f32[1024,128]{0,1:T(8,128)S(1)} fusion(f32[8,4,64,1024]{3,2,1,0:T(8,128)} %param.5, f32[64,128]{1,0:T(8,128)} %four_ref.1, f32[8,4,128]{2,1,0:T(4,128)S(1)} %broadcast_multiply_fusion), kind=kOutput, calls=%fused_computation | convolution fusion | flops 3221487616 | bytes 8962048 | tf_op jit(solution)/shard_map/dot_general | solution.py:67
  9.0 0.4 reshape.29
  9.5 0.5 constant_dynamic-slice_fusion.4
  9.9 0.1 copy.8
  10.1 3.3 %collective-permute-start = (f32[520,128]{1,0:T(8,128)S(1)}, f32[520,128]{1,0:T(8,128)S(1)}, u32[]{:S(2)}, u32[]{:S(2)}) collective-permute-start(f32[520,128]{1,0:T(8,128)S(1)} %pad_maximum_fusion.2), channel_id=1, source_target_pairs={{0,1},{1,0},{2,3},{3,2},{4,5},{5,4},{6,7},{7,6},{8,9},{9,8},{10,11... | collective-permute-start | bytes 798728 | tf_op jit(solution)/shard_map/ppermute | solution.py:70
  13.4 0.1 copy.7
  13.6 1.0 %collective-permute-done = f32[520,128]{1,0:T(8,128)S(1)} collective-permute-done((f32[520,128]{1,0:T(8,128)S(1)}, f32[520,128]{1,0:T(8,128)S(1)}, u32[]{:S(2)}, u32[]{:S(2)}) %collective-permute-start) | collective-permute-done | bytes 266272 | tf_op jit(solution)/shard_map/ppermute | solution.py:70
  14.7 13.7 %all_to_all.15 = f32[16,40,128]{2,1,0:T(8,128)S(1)} all-to-all(f32[16,40,128]{2,1,0:T(8,128)S(1)} %pad_maximum_fusion.1), channel_id=1, replica_groups=mesh['y'=4,'xh'=2,'z'=8,'xl'=2,'c'=2] {'y','xh','xl'}, dimensions={0} | all-to-all | bytes 655360 | tf_op jit(solution)/shard_map/all_to_all | solution.py:85
  28.4 0.7 %broadcast_in_dim.5 = f32[8,48,128]{2,1,0:T(8,128)} broadcast(f32[48,128]{1,0:T(8,128)S(1)} %pad_maximum_fusion.3), dimensions={1,2} | broadcast | bytes 221184 | tf_op jit(solution)/shard_map/broadcast_in_dim | solution.py:91
  29.1 8.2 %all-to-all-start.1 = ((f32[8,48,128]{2,1,0:T(8,128)}), f32[8,48,128]{2,1,0:T(8,128)S(1)}, u32[]{:S(2)}, u32[]{:S(2)}) async-start(f32[8,48,128]{2,1,0:T(8,128)} %broadcast_in_dim.5), calls=%async_computation.1 | async-start | bytes 393216 | tf_op jit(solution)/shard_map/all_to_all | solution.py:90
  37.3 0.6 constant_dynamic-slice_fusion.old_ref
  37.9 0.6 slice.24
  38.5 7.5 %all-to-all-done.1.parts_ref = f32[8,48,128]{2,1,0:T(8,128)S(1)} async-done(((f32[8,48,128]{2,1,0:T(8,128)}), f32[8,48,128]{2,1,0:T(8,128)S(1)}, u32[]{:S(2)}, u32[]{:S(2)}) %all-to-all-start.1) | async-done | bytes 196640 | tf_op jit(solution)/shard_map/all_to_all | solution.py:90
  46.0 0.7 copy-done.2
  46.7 3.8 %hals.1 = f32[16,32,128]{2,1,0:T(8,128)} custom-call(f32[8,48,128]{2,1,0:T(8,128)} %copy-done.2, f32[64,128]{1,0:T(8,128)} %bitcast.23, f32[64,128]{1,0:T(8,128)} %four_ref.1, f32[32,128]{1,0:T(8,128)} %constant_dynamic-slice_fusion.old_ref), custom_call_target="tpu_custom_call" | custom-call | tf_op jit(solution)/shard_map/hals/pallas_call | solution.py:94
  50.4 11.1 %all_to_all.16 = f32[16,32,128]{2,1,0:T(8,128)S(1)} all-to-all(f32[16,32,128]{2,1,0:T(8,128)} %hals.1), channel_id=1, replica_groups=mesh['y'=4,'xh'=2,'z'=8,'xl'=2,'c'=2] {'y','xh','xl'}, dimensions={0} | all-to-all | bytes 524288 | tf_op jit(solution)/shard_map/all_to_all | solution.py:99
  61.5 4.0 %collective-permute-start.1 = (f32[512,128]{1,0:T(8,128)S(1)}, f32[512,128]{1,0:T(8,128)S(1)}, u32[]{:S(2)}, u32[]{:S(2)}) collective-permute-start(f32[512,128]{1,0:T(8,128)S(1)} %bitcast.22), channel_id=1, source_target_pairs={{0,1},{1,0},{2,3},{3,2},{4,5},{5,4},{6,7},{7,6},{8,9},{9,8},{10,11... | collective-permute-start | bytes 786440 | tf_op jit(solution)/shard_map/ppermute | solution.py:100
  65.5 1.2 %collective-permute-done.1 = f32[512,128]{1,0:T(8,128)S(1)} collective-permute-done((f32[512,128]{1,0:T(8,128)S(1)}, f32[512,128]{1,0:T(8,128)S(1)}, u32[]{:S(2)}, u32[]{:S(2)}) %collective-permute-start.1) | collective-permute-done | bytes 262176 | tf_op jit(solution)/shard_map/ppermute | solution.py:100
  66.7 0.0 copy-start.1
  66.7 1.7 %fusion.3 = f32[128,128]{1,0:T(8,128)} fusion(f32[1024,128]{1,0:T(8,128)S(1)} %pad_maximum_fusion), kind=kOutput, calls=%fused_computation.19 | convolution fusion | flops 201326592 | bytes 589824 | tf_op jit(solution)/shard_map/dot_general | solution.py:104
  (19 shorter events, 0.3 us)
Async XLA Ops:
  0.6 36.7 %copy-start = (f32[1024,128]{1,0:T(8,128)S(1)}, f32[1024,128]{1,0:T(8,128)}, u32[]{:S(2)}) copy-start(f32[1024,128]{1,0:T(8,128)} %param.6) | copy-start | bytes 1572868
  0.6 12.9 %copy-start.4 = (f32[8,128]{1,0:T(8,128)S(1)}, f32[8,128]{1,0:T(8,128)}, u32[]{:S(2)}) copy-start(f32[8,128]{1,0:T(8,128)} %param.7) | copy-start | bytes 12292
  0.7 9.4 %copy-start.3 = (f32[4,128]{1,0:T(4,128)S(1)}, f32[4,128]{1,0:T(4,128)}, u32[]{:S(2)}) copy-start(f32[4,128]{1,0:T(4,128)} %param.8) | copy-start | bytes 6148
  10.1 4.5 %collective-permute-start = (f32[520,128]{1,0:T(8,128)S(1)}, f32[520,128]{1,0:T(8,128)S(1)}, u32[]{:S(2)}, u32[]{:S(2)}) collective-permute-start(f32[520,128]{1,0:T(8,128)S(1)} %pad_maximum_fusion.2), channel_id=1, source_target_pairs={{0,1},{1,0},{2,3},{3,2},{4,5},{5,4},{6,7},{7,6},{8,9},{9,8},{10,11... | collective-permute-start | bytes 798728 | tf_op jit(solution)/shard_map/ppermute | solution.py:70
  29.1 16.9 %all-to-all-start.1 = ((f32[8,48,128]{2,1,0:T(8,128)}), f32[8,48,128]{2,1,0:T(8,128)S(1)}, u32[]{:S(2)}, u32[]{:S(2)}) async-start(f32[8,48,128]{2,1,0:T(8,128)} %broadcast_in_dim.5), calls=%async_computation.1 | async-start | bytes 393216 | tf_op jit(solution)/shard_map/all_to_all | solution.py:90
  46.0 0.7 copy-start.2
  61.5 5.2 %collective-permute-start.1 = (f32[512,128]{1,0:T(8,128)S(1)}, f32[512,128]{1,0:T(8,128)S(1)}, u32[]{:S(2)}, u32[]{:S(2)}) collective-permute-start(f32[512,128]{1,0:T(8,128)S(1)} %bitcast.22), channel_id=1, source_target_pairs={{0,1},{1,0},{2,3},{3,2},{4,5},{5,4},{6,7},{7,6},{8,9},{9,8},{10,11... | collective-permute-start | bytes 786440 | tf_op jit(solution)/shard_map/ppermute | solution.py:100
  66.7 1.7 %copy-start.1 = (f32[1024,128]{1,0:T(8,128)}, f32[1024,128]{1,0:T(8,128)S(1)}, u32[]{:S(2)}) copy-start(f32[1024,128]{1,0:T(8,128)S(1)} %pad_maximum_fusion) | copy-start | bytes 1572868

commit v2 on v1

--- a/solution.py
+++ b/solution.py
@@ -2,10 +2,168 @@
 import jax.numpy as jnp
 from jax import lax
 from jax.experimental import pallas as pl
+from jax.experimental.pallas import tpu as pltpu
 from jax.sharding import Mesh, PartitionSpec as P
 
 HIGHEST = lax.Precision.HIGHEST
 PLANE = ("y", "xh", "xl")
+IN_VMEM = pl.BlockSpec(memory_space=pltpu.VMEM)
+IN_PLACE = pl.BlockSpec(memory_space=pl.ANY)
+
+
+def in_vmem(value):
+    return pltpu.with_memory_space_constraint(value, pltpu.VMEM)
+
+
+def split(value):
+    high = value.astype(jnp.bfloat16)
+    low = (value - high.astype(jnp.float32)).astype(jnp.bfloat16)
+    return high, low
+
+
+CHUNKS = 4
+IN_FLIGHT = 4
+
+
+def contract_kernel(
+    flat_ref, one_hbm, two_hbm, three_hbm, four_hbm, send_ref, keep_ref, old_ref, gram_ref,
+    buf, khatri, two_ref, three_ref, four_ref, sems, small_sems,
+):
+    depth, width = buf.shape[2:]
+    rows = old_ref.shape[0]
+    rank = gram_ref.shape[0]
+    core = lax.axis_index("c")
+    start = core * width + lax.axis_index(PLANE) * rows
+    small = [
+        pltpu.make_async_copy(source, target, small_sems.at[n])
+        for n, (source, target) in enumerate(
+            (
+                (two_hbm, two_ref),
+                (three_hbm, three_ref),
+                (four_hbm, four_ref),
+                (one_hbm.at[pl.ds(pl.multiple_of(start, rows), rows), :], old_ref),
+            )
+        )
+    ]
+    for copy in small[:3]:
+        copy.start()
+    copies = []
+    for part in range(2):
+        side = (1 - core) if part == 0 else core
+        for q in range(CHUNKS):
+            copies.append(
+                pltpu.make_async_copy(
+                    flat_ref.at[pl.ds(q * depth, depth), pl.ds(pl.multiple_of(side * width, width), width)],
+                    buf.at[part, q],
+                    sems.at[part, q],
+                )
+            )
+    for copy in copies[:IN_FLIGHT]:
+        copy.start()
+    small[3].start()
+    for copy in small[:3]:
+        copy.wait()
+    four = four_ref[...]
+    pairs = two_ref.shape[0] * three_ref.shape[0]
+    for q in range(CHUNKS):
+        blocks = []
+        for p in range(q * pairs // CHUNKS, (q + 1) * pairs // CHUNKS):
+            i, j = divmod(p, three_ref.shape[0])
+            blocks.append((two_ref[i : i + 1, :] * three_ref[j : j + 1, :]) * four)
+        high, low = split(jnp.concatenate(blocks, axis=0).T)
+        khatri[q] = jnp.concatenate([high, low], axis=0)
+    gram_ref[...] = transposed_dot(four, four)
+    send_ref[width : width + three_ref.shape[0], :] = three_ref[...]
+    send_ref[width + three_ref.shape[0] :, :] = jnp.zeros_like(three_ref)
+    for part, out_ref in ((0, send_ref), (1, keep_ref)):
+        both = jnp.zeros((2 * rank, width), jnp.float32)
+        cross = jnp.zeros((rank, width), jnp.float32)
+        for q in range(CHUNKS):
+            n = part * CHUNKS + q
+            copies[n].wait()
+            if n + IN_FLIGHT < len(copies):
+                copies[n + IN_FLIGHT].start()
+            high, low = split(buf[part, q])
+            both = both + jnp.dot(khatri[q], high, preferred_element_type=jnp.float32)
+            cross = cross + jnp.dot(khatri[q, :rank], low, preferred_element_type=jnp.float32)
+        out_ref[:width, :] = (both[:rank] + (both[rank:] + cross)).T
+    small[3].wait()
+
+
+def contract(flat, one, two, three, four, half, rows):
+    rank = four.shape[1]
+    depth = flat.shape[0] // CHUNKS
+    return pl.pallas_call(
+        contract_kernel,
+        out_shape=(
+            pltpu.VMEM((half + 2 * three.shape[0], rank), jnp.float32),
+            pltpu.VMEM((half, rank), jnp.float32),
+            pltpu.VMEM((rows, rank), jnp.float32),
+            pltpu.VMEM((rank, rank), jnp.float32),
+        ),
+        in_specs=[IN_PLACE] * 5,
+        out_specs=(IN_VMEM,) * 4,
+        scratch_shapes=[
+            pltpu.VMEM((2, CHUNKS, depth, half), jnp.float32),
+            pltpu.VMEM((CHUNKS, 2 * rank, depth), jnp.bfloat16),
+            pltpu.VMEM(two.shape, jnp.float32),
+            pltpu.VMEM(three.shape, jnp.float32),
+            pltpu.VMEM(four.shape, jnp.float32),
+            pltpu.SemaphoreType.DMA((2, CHUNKS)),
+            pltpu.SemaphoreType.DMA((4,)),
+        ],
+        name="contract",
+    )(flat, one, two, three, four)
+
+
+def own_gram(value):
+    rank = value.shape[1]
+    high, low = split(value)
+    both = lax.dot_general(
+        high,
+        jnp.concatenate([high, low], axis=1),
+        (((0,), (0,)), ((), ())),
+        preferred_element_type=jnp.float32,
+    )
+    cross = both[:, rank:]
+    return both[:, :rank] + (cross + cross.T)
+
+
+def half_gram_kernel(mine_ref, gram_ref):
+    gram_ref[...] = own_gram(mine_ref[...])
+
+
+def half_gram(mine):
+    rank = mine.shape[1]
+    return pl.pallas_call(
+        half_gram_kernel,
+        out_shape=pltpu.VMEM((rank, rank), jnp.float32),
+        in_specs=[IN_VMEM],
+        out_specs=IN_VMEM,
+        name="half_gram",
+    )(in_vmem(mine))
+
+
+def finish_kernel(mine_ref, other_ref, part_ref, new_ref, gram_ref):
+    core = lax.axis_index("c")
+    half = mine_ref.shape[0]
+    new_ref[pl.ds(pl.multiple_of(core * half, half), half), :] = mine_ref[...]
+    new_ref[pl.ds(pl.multiple_of((1 - core) * half, half), half), :] = other_ref[...]
+    gram_ref[...] = part_ref[...] + own_gram(other_ref[...])
+
+
+def finish(mine, other, part):
+    half, rank = mine.shape
+    return pl.pallas_call(
+        finish_kernel,
+        out_shape=(
+            jax.ShapeDtypeStruct((2 * half, rank), jnp.float32),
+            jax.ShapeDtypeStruct((rank, rank), jnp.float32),
+        ),
+        in_specs=[IN_VMEM] * 3,
+        out_specs=(IN_VMEM, IN_VMEM),
+        name="finish",
+    )(in_vmem(mine), in_vmem(other), in_vmem(part))
 
 
 def transposed_dot(a, b):
@@ -14,16 +172,14 @@
     )
 
 
-def hals_kernel(parts_ref, two_ref, four_ref, old_ref, out_ref):
-    rank = old_ref.shape[1]
-    rows = old_ref.shape[0]
+def hals_kernel(parts_ref, got_ref, gram_ref, old_ref, out_ref):
+    rows, rank = old_ref.shape
     mttkrp = parts_ref[0, :rows, :]
     for z in range(1, parts_ref.shape[0]):
         mttkrp = mttkrp + parts_ref[z, :rows, :]
     three = parts_ref[:, rows:, :].reshape(-1, rank)
-    two = two_ref[...]
-    four = four_ref[...]
-    gram = transposed_dot(two, two) * transposed_dot(three, three) * transposed_dot(four, four)
+    two = got_ref[:, rows : rows + 4, :].reshape(-1, rank)
+    gram = transposed_dot(two, two) * transposed_dot(three, three) * gram_ref[...]
     row = lax.broadcasted_iota(jnp.int32, (rank, rank), 0)
     col = lax.broadcasted_iota(jnp.int32, (rank, rank), 1)
     diag = jnp.where(row == col, gram, 0.0)
@@ -56,23 +212,14 @@
     depth = lax.axis_size("z")
     half = mode_one // cores
     rows = half // plane
-    core = lax.axis_index("c")
     plane_pos = lax.axis_index(PLANE)
-    khatri = (
-        factor_two[:, None, None, :]
-        * factor_three[None, :, None, :]
-        * factor_four[None, None, :, :]
-    ).reshape(-1, rank)
     flat = tensor.reshape(-1, mode_one)
-    partial = lax.dot_general(flat, khatri, (((0,), (0,)), ((), ())), precision=HIGHEST)
-    partial = partial.reshape(cores, half, rank)
+    send, keep, old, gram_four = contract(
+        flat, factor_one, factor_two, factor_three, factor_four, half, rows
+    )
     swap = [(0, 1), (1, 0)]
-    other = lax.ppermute(
-        jnp.concatenate([lax.dynamic_index_in_dim(partial, 1 - core, 0, False), factor_three, factor_three], axis=0),
-        "c",
-        swap,
-    )
-    mine = lax.dynamic_index_in_dim(partial, core, 0, False) + other[:half]
+    other = lax.ppermute(send, "c", swap)
+    mine = keep + other[:half]
     pair_three = jnp.concatenate([factor_three, other[half : half + 4]], axis=0)
     xl = lax.axis_index("xl")
     seg = plane_pos // 2
@@ -84,25 +231,22 @@
     )
     got = lax.all_to_all(blocks, PLANE, 0, 0, tiled=True)
     own = jnp.sum(got[:, :rows], axis=0)
-    two = got[:, rows : rows + 4].reshape(-1, rank)
     three = got[:, rows + 4]
     block = jnp.concatenate([own, three], axis=0)
     parts = lax.all_to_all(
         jnp.broadcast_to(block[None], (depth, *block.shape)), "z", 0, 0, tiled=True
     )
-    old = lax.dynamic_slice_in_dim(factor_one, core * half + plane_pos * rows, rows, 0)
     spread = pl.pallas_call(
         hals_kernel,
-        out_shape=jax.ShapeDtypeStruct((plane, rows, rank), jnp.float32),
+        out_shape=pltpu.VMEM((plane, rows, rank), jnp.float32),
+        in_specs=[IN_VMEM] * 4,
+        out_specs=IN_VMEM,
         name="hals",
-    )(parts, two, factor_four, old)
+    )(*(in_vmem(v) for v in (parts, got, gram_four, old)))
     mine_new = lax.all_to_all(spread, PLANE, 0, 0, tiled=True).reshape(half, rank)
     other_new = lax.ppermute(mine_new, "c", swap)
-    first = jnp.where(core == 0, mine_new, other_new)
-    second = jnp.where(core == 0, other_new, mine_new)
-    new_factor = jnp.concatenate([first, second], axis=0)
-    factor_gram = jnp.dot(new_factor.T, new_factor, precision=HIGHEST)
-    return (new_factor, factor_gram)
+    part_gram = half_gram(mine_new)
+    return finish(mine_new, other_new, part_gram)
 
 
 def solution(mesh):

time: 68.7 us -> 59.5 us (0.87)
  blocking collectives: 24.7 us -> 40.7 us
  matrix products: 9.23 us -> 0 us
  starting transfers between devices: 15.5 us -> 7.48 us
  waiting for transfers between devices: 9.62 us -> 2.02 us
  Pallas kernels: 3.76 us -> 8.18 us
  local copies, waits for them, and re-layouts: 3.82 us -> 0.08 us
  other arithmetic: 0.97 us -> 0.09 us
    all_to_all x0 -> x1, blocking collectives: none -> 16.7 us  [per_device(): lax.all_to_all(jnp.broadcast_to(block[None], (depth, *block.shape)), 'z',...]
    dot_general x2 -> x0, matrix products: 9.23 us -> none  [the longest x1 7.56 us: per_device(): lax.dot_general(flat, khatri, (((0,), (0,)), ((), ())), precision=HIGHEST)]
    all_to_all x1 -> x0, starting transfers between devices: 8.19 us -> none  [per_device(): lax.all_to_all(jnp.broadcast_to(block[None], (depth, *block.shape)), 'z',...]
    all_to_all x1 -> x0, waiting for transfers between devices: 7.46 us -> none  [per_device(): lax.all_to_all(jnp.broadcast_to(block[None], (depth, *block.shape)), 'z',...]
    pallas_call x1 -> x4, Pallas kernels: 3.76 us -> 8.18 us  [the longest x1 4.84 us: contract(): pl.pallas_call(contract_kernel, out_shape=(pltpu.VMEM((half + 2 * three.s...]
    dynamic_slice x4 -> x0, local copies, waits for them, and re-layouts: 1.32 us -> none  [the longest x1 0.6 us: per_device(): lax.dynamic_slice_in_dim(factor_one, core * half + plane_pos * rows, rows...]
    mul x1 -> x0, other arithmetic: 0.77 us -> none  [per_device(): factor_two[:, None, None, :] * factor_three[None, :, None, :]]
    all_to_all x1, blocking collectives: 11.1 us -> 10.3 us  [per_device(): lax.all_to_all(spread, PLANE, 0, 0, tiled=True).reshape(half, rank)]
  transfers between devices with their start and end apart: 3 -> 2, of which waited for: 3 -> 2; matrix products, arithmetic and copies ran while one was open for 2% -> 0% of each run, Pallas kernels for 0% -> 0%
where the time goes in v2:
time: 59.5 us; the launch traced here: 59.2 us
  blocking collectives  40.7 us (68%)
  Pallas kernels  8.18 us (14%)
  starting transfers between devices  7.48 us (13%)
  waiting for transfers between devices  2.02 us (3%)
  between operations  0.73 us (1%)
    all_to_all x1, blocking collectives, per_device(): lax.all_to_all(jnp.broadcast_to(block[None], (depth, *block.shape)), 'z',...  16.7 us
    all_to_all x1, blocking collectives, per_device(): got = lax.all_to_all(blocks, PLANE, 0, 0, tiled=True)  13.7 us
    all_to_all x1, blocking collectives, per_device(): lax.all_to_all(spread, PLANE, 0, 0, tiled=True).reshape(half, rank)  10.3 us
    pallas_call x1, Pallas kernels, contract(): pl.pallas_call(contract_kernel, out_shape=(pltpu.VMEM((half + 2 * three.s...  4.84 us
    ppermute x1, starting transfers between devices, per_device(): other_new = lax.ppermute(mine_new, 'c', swap)  4.2 us
    ppermute x1, starting transfers between devices, per_device(): other = lax.ppermute(send, 'c', swap)  3.28 us
    pallas_call x1, Pallas kernels, per_device(): pl.pallas_call(hals_kernel, out_shape=pltpu.VMEM((plane, rows, rank), jnp...  2 us
  transfers between devices with their start and end apart: 2, of which 2 were waited for; matrix products, arithmetic and copies ran while one was open for 0% of the time, Pallas kernels for 0%

profile of v2, /device:TPU:1, one launch (start us, length us, event | category | flops | bytes accessed | tf_op | source)
XLA Modules:
  0.0 59.2 jit_solution(2465504101294067593)
XLA Ops:
  0.6 0.0 copy-start.1
  0.6 0.0 copy-start
  0.7 4.8 %contract.1 = (f32[520,128]{1,0:T(8,128)S(1)}, f32[512,128]{1,0:T(8,128)S(1)}, f32[32,128]{1,0:T(8,128)S(1)}, f32[128,128]{1,0:T(8,128)S(1)}) custom-call(f32[2048,1024]{1,0:T(8,128)} %bitcast.7, f32[1024,128]{1,0:T(8,128)} %one_hbm.1, f32[8,128]{1,0:T(8,128)} %two_hbm.1, f32[4,128]{1,0:T(4,128)} %three_hbm.1, f32[64,128]{1,0:T(8,128)} %four_hbm.1), custom_call_target="tpu_custom_call" | custom-call | tf_op jit(solution)/shard_map/contract/pallas_call | solution.py:96
  5.5 3.3 %collective-permute-start = (f32[520,128]{1,0:T(8,128)S(1)}, f32[520,128]{1,0:T(8,128)S(1)}, u32[]{:S(2)}, u32[]{:S(2)}) collective-permute-start(f32[520,128]{1,0:T(8,128)S(1)} %get-tuple-element.7), channel_id=1, source_target_pairs={{0,1},{1,0},{2,3},{3,2},{4,5},{5,4},{6,7},{7,6},{8,9},{9,8},{10,11... | collective-permute-start | bytes 798728 | tf_op jit(solution)/shard_map/ppermute | solution.py:221
  8.8 0.0 copy-done
  8.8 1.2 %collective-permute-done = f32[520,128]{1,0:T(8,128)S(1)} collective-permute-done((f32[520,128]{1,0:T(8,128)S(1)}, f32[520,128]{1,0:T(8,128)S(1)}, u32[]{:S(2)}, u32[]{:S(2)}) %collective-permute-start) | collective-permute-done | bytes 266272 | tf_op jit(solution)/shard_map/ppermute | solution.py:221
  10.0 0.0 copy-done.1
  10.1 13.7 %all_to_all.15.got_ref = f32[16,40,128]{2,1,0:T(8,128)S(1)} all-to-all(f32[16,40,128]{2,1,0:T(8,128)S(1)} %pad_maximum_fusion), channel_id=1, replica_groups=mesh['y'=4,'xh'=2,'z'=8,'xl'=2,'c'=2] {'y','xh','xl'}, dimensions={0} | all-to-all | bytes 655360 | tf_op jit(solution)/shard_map/all_to_all | solution.py:232
  23.8 16.7 %all_to_all.16.parts_ref = f32[8,48,128]{2,1,0:T(8,128)S(1)} all-to-all(f32[8,48,128]{2,1,0:T(8,128)S(1)} %broadcast_in_dim.5), channel_id=1, replica_groups=mesh['y'=4,'xh'=2,'z'=8,'xl'=2,'c'=2] {'z'}, dimensions={0} | all-to-all | bytes 393216 | tf_op jit(solution)/shard_map/all_to_all | solution.py:236
  40.5 2.0 %hals.1 = f32[16,32,128]{2,1,0:T(8,128)S(1)} custom-call(f32[8,48,128]{2,1,0:T(8,128)S(1)} %all_to_all.16.parts_ref, f32[16,40,128]{2,1,0:T(8,128)S(1)} %all_to_all.15.got_ref, f32[128,128]{1,0:T(8,128)S(1)} %get-tuple-element.8.gram_ref, f32[32,128]{1,0:T(8,128)S(1)} %get-tuple-element.9.old_ref), custom_call_target="tpu_custom_call" | custom-call | tf_op jit(solution)/shard_map/hals/pallas_call | solution.py:239
  42.5 10.3 %all_to_all.17 = f32[16,32,128]{2,1,0:T(8,128)S(1)} all-to-all(f32[16,32,128]{2,1,0:T(8,128)S(1)} %hals.1), channel_id=1, replica_groups=mesh['y'=4,'xh'=2,'z'=8,'xl'=2,'c'=2] {'y','xh','xl'}, dimensions={0} | all-to-all | bytes 524288 | tf_op jit(solution)/shard_map/all_to_all | solution.py:246
  52.8 4.2 %collective-permute-start.1 = (f32[512,128]{1,0:T(8,128)S(1)}, f32[512,128]{1,0:T(8,128)S(1)}, u32[]{:S(2)}, u32[]{:S(2)}) collective-permute-start(f32[512,128]{1,0:T(8,128)S(1)} %bitcast.4), channel_id=1, source_target_pairs={{0,1},{1,0},{2,3},{3,2},{4,5},{5,4},{6,7},{7,6},{8,9},{9,8},{10,11... | collective-permute-start | bytes 786440 | tf_op jit(solution)/shard_map/ppermute | solution.py:247
  57.0 0.3 half_gram.1.part_ref
  57.3 0.9 %collective-permute-done.1.other_ref = f32[512,128]{1,0:T(8,128)S(1)} collective-permute-done((f32[512,128]{1,0:T(8,128)S(1)}, f32[512,128]{1,0:T(8,128)S(1)}, u32[]{:S(2)}, u32[]{:S(2)}) %collective-permute-start.1) | collective-permute-done | bytes 262176 | tf_op jit(solution)/shard_map/ppermute | solution.py:247
  58.2 1.1 %finish.1 = (f32[1024,128]{1,0:T(8,128)}, f32[128,128]{1,0:T(8,128)}) custom-call(f32[512,128]{1,0:T(8,128)S(1)} %bitcast.6, f32[512,128]{1,0:T(8,128)S(1)} %collective-permute-done.1.other_ref, f32[128,128]{1,0:T(8,128)S(1)} %half_gram.1.part_ref), custom_call_target="tpu_custom_call" | custom-call | tf_op jit(solution)/shard_map/finish/pallas_call | solution.py:157
  (12 shorter events, 0.2 us)
Async XLA Ops:
  0.6 9.3 %copy-start.1 = (f32[4,128]{1,0:T(4,128)S(1)}, f32[4,128]{1,0:T(4,128)}, u32[]{:S(2)}) copy-start(f32[4,128]{1,0:T(4,128)} %three_hbm.1) | copy-start | bytes 6148
  0.6 8.1 %copy-start = (f32[8,128]{1,0:T(8,128)S(1)}, f32[8,128]{1,0:T(8,128)}, u32[]{:S(2)}) copy-start(f32[8,128]{1,0:T(8,128)} %two_hbm.1) | copy-start | bytes 12292
  5.5 4.5 %collective-permute-start = (f32[520,128]{1,0:T(8,128)S(1)}, f32[520,128]{1,0:T(8,128)S(1)}, u32[]{:S(2)}, u32[]{:S(2)}) collective-permute-start(f32[520,128]{1,0:T(8,128)S(1)} %get-tuple-element.7), channel_id=1, source_target_pairs={{0,1},{1,0},{2,3},{3,2},{4,5},{5,4},{6,7},{7,6},{8,9},{9,8},{10,11... | collective-permute-start | bytes 798728 | tf_op jit(solution)/shard_map/ppermute | solution.py:221
  52.8 5.4 %collective-permute-start.1 = (f32[512,128]{1,0:T(8,128)S(1)}, f32[512,128]{1,0:T(8,128)S(1)}, u32[]{:S(2)}, u32[]{:S(2)}) collective-permute-start(f32[512,128]{1,0:T(8,128)S(1)} %bitcast.4), channel_id=1, source_target_pairs={{0,1},{1,0},{2,3},{3,2},{4,5},{5,4},{6,7},{7,6},{8,9},{9,8},{10,11... | collective-permute-start | bytes 786440 | tf_op jit(solution)/shard_map/ppermute | solution.py:247

commit v3 on v2

--- a/solution.py
+++ b/solution.py
@@ -7,6 +7,7 @@
 
 HIGHEST = lax.Precision.HIGHEST
 PLANE = ("y", "xh", "xl")
+Z_MASKS = (7, 1, 2)
 IN_VMEM = pl.BlockSpec(memory_space=pltpu.VMEM)
 IN_PLACE = pl.BlockSpec(memory_space=pl.ANY)
 
@@ -172,12 +173,21 @@
     )
 
 
-def hals_kernel(parts_ref, got_ref, gram_ref, old_ref, out_ref):
+def hals_kernel(block_ref, peer_ref, got_ref, gram_ref, old_ref, out_ref, three_ref):
     rows, rank = old_ref.shape
-    mttkrp = parts_ref[0, :rows, :]
-    for z in range(1, parts_ref.shape[0]):
-        mttkrp = mttkrp + parts_ref[z, :rows, :]
-    three = parts_ref[:, rows:, :].reshape(-1, rank)
+    here = lax.axis_index("z")
+    held = [0]
+    for mask in Z_MASKS[:-1]:
+        held += [mask ^ other for other in held]
+    size = (block_ref.shape[0] - rows) // len(held)
+    for ref, mask in ((block_ref, 0), (peer_ref, Z_MASKS[-1])):
+        for n, other in enumerate(held):
+            z = jnp.bitwise_xor(here, mask ^ other)
+            three_ref[pl.ds(pl.multiple_of(z * size, size), size), :] = ref[
+                rows + n * size : rows + (n + 1) * size, :
+            ]
+    mttkrp = block_ref[:rows, :] + peer_ref[:rows, :]
+    three = three_ref[...]
     two = got_ref[:, rows : rows + 4, :].reshape(-1, rank)
     gram = transposed_dot(two, two) * transposed_dot(three, three) * gram_ref[...]
     row = lax.broadcasted_iota(jnp.int32, (rank, rank), 0)
@@ -232,17 +242,20 @@
     got = lax.all_to_all(blocks, PLANE, 0, 0, tiled=True)
     own = jnp.sum(got[:, :rows], axis=0)
     three = got[:, rows + 4]
-    block = jnp.concatenate([own, three], axis=0)
-    parts = lax.all_to_all(
-        jnp.broadcast_to(block[None], (depth, *block.shape)), "z", 0, 0, tiled=True
-    )
+    for mask in Z_MASKS:
+        block = jnp.concatenate([own, three], axis=0)
+        peer = lax.ppermute(block, "z", [(i, i ^ mask) for i in range(depth)])
+        if mask != Z_MASKS[-1]:
+            own = own + peer[:rows]
+            three = jnp.concatenate([three, peer[rows:]], axis=0)
     spread = pl.pallas_call(
         hals_kernel,
         out_shape=pltpu.VMEM((plane, rows, rank), jnp.float32),
-        in_specs=[IN_VMEM] * 4,
+        in_specs=[IN_VMEM] * 5,
         out_specs=IN_VMEM,
+        scratch_shapes=[pltpu.VMEM((2 * three.shape[0], rank), jnp.float32)],
         name="hals",
-    )(*(in_vmem(v) for v in (parts, got, gram_four, old)))
+    )(*(in_vmem(v) for v in (block, peer, got, gram_four, old)))
     mine_new = lax.all_to_all(spread, PLANE, 0, 0, tiled=True).reshape(half, rank)
     other_new = lax.ppermute(mine_new, "c", swap)
     part_gram = half_gram(mine_new)

time: 59.5 us -> 58.1 us (0.976)
  blocking collectives: 40.7 us -> 24 us
  starting transfers between devices: 7.48 us -> 18.4 us
  waiting for transfers between devices: 2.02 us -> 6.48 us
    all_to_all x1 -> x0, blocking collectives: 16.7 us -> none  [per_device(): lax.all_to_all(jnp.broadcast_to(block[None], (depth, *block.shape)), 'z',...]
    ppermute x0 -> x3, starting transfers between devices: none -> 9.37 us  [per_device(): peer = lax.ppermute(block, 'z', [(i, i ^ mask) for i in range(depth)])]
    ppermute x0 -> x3, waiting for transfers between devices: none -> 4.46 us  [per_device(): peer = lax.ppermute(block, 'z', [(i, i ^ mask) for i in range(depth)])]
    ppermute x1, starting transfers between devices: 4.2 us -> 5.72 us  [per_device(): other_new = lax.ppermute(mine_new, 'c', swap)]
  transfers between devices with their start and end apart: 2 -> 5, of which waited for: 2 -> 5; matrix products, arithmetic and copies ran while one was open for 0% -> 0% of each run, Pallas kernels for 0% -> 1%
where the time goes in v3:
time: 58.1 us; the launch traced here: 58 us
  blocking collectives  24 us (41%)
  starting transfers between devices  18.4 us (32%)
  Pallas kernels  8.18 us (14%)
  waiting for transfers between devices  6.48 us (11%)
  between operations  0.73 us (1%)
    all_to_all x1, blocking collectives, per_device(): got = lax.all_to_all(blocks, PLANE, 0, 0, tiled=True)  13.7 us
    all_to_all x1, blocking collectives, per_device(): lax.all_to_all(spread, PLANE, 0, 0, tiled=True).reshape(half, rank)  10.3 us
    ppermute x3, starting transfers between devices, per_device(): peer = lax.ppermute(block, 'z', [(i, i ^ mask) for i in range(depth)])  9.37 us
    ppermute x1, starting transfers between devices, per_device(): other_new = lax.ppermute(mine_new, 'c', swap)  5.72 us
    pallas_call x1, Pallas kernels, contract(): pl.pallas_call(contract_kernel, out_shape=(pltpu.VMEM((half + 2 * three.s...  4.84 us
    ppermute x3, waiting for transfers between devices, per_device(): peer = lax.ppermute(block, 'z', [(i, i ^ mask) for i in range(depth)])  4.46 us
    ppermute x1, starting transfers between devices, per_device(): other = lax.ppermute(send, 'c', swap)  3.28 us
    pallas_call x1, Pallas kernels, per_device(): pl.pallas_call(hals_kernel, out_shape=pltpu.VMEM((plane, rows, rank), jnp...  1.99 us
  transfers between devices with their start and end apart: 5, of which 5 were waited for; matrix products, arithmetic and copies ran while one was open for 0% of the time, Pallas kernels for 1%

profile of v3, /device:TPU:1, one launch (start us, length us, event | category | flops | bytes accessed | tf_op | source)
XLA Modules:
  0.0 58.0 jit_solution(14769065514280132253)
XLA Ops:
  0.6 0.0 copy-start.1
  0.6 0.0 copy-start
  0.7 4.8 %contract.1 = (f32[520,128]{1,0:T(8,128)S(1)}, f32[512,128]{1,0:T(8,128)S(1)}, f32[32,128]{1,0:T(8,128)S(1)}, f32[128,128]{1,0:T(8,128)S(1)}) custom-call(f32[2048,1024]{1,0:T(8,128)} %bitcast.7, f32[1024,128]{1,0:T(8,128)} %one_hbm.1, f32[8,128]{1,0:T(8,128)} %two_hbm.1, f32[4,128]{1,0:T(4,128)} %three_hbm.1, f32[64,128]{1,0:T(8,128)} %four_hbm.1), custom_call_target="tpu_custom_call" | custom-call | tf_op jit(solution)/shard_map/contract/pallas_call | solution.py:97
  5.5 3.3 %collective-permute-start = (f32[520,128]{1,0:T(8,128)S(1)}, f32[520,128]{1,0:T(8,128)S(1)}, u32[]{:S(2)}, u32[]{:S(2)}) collective-permute-start(f32[520,128]{1,0:T(8,128)S(1)} %get-tuple-element.7), channel_id=1, source_target_pairs={{0,1},{1,0},{2,3},{3,2},{4,5},{5,4},{6,7},{7,6},{8,9},{9,8},{10,11... | collective-permute-start | bytes 798728 | tf_op jit(solution)/shard_map/ppermute | solution.py:231
  8.8 0.0 copy-done
  8.8 1.2 %collective-permute-done = f32[520,128]{1,0:T(8,128)S(1)} collective-permute-done((f32[520,128]{1,0:T(8,128)S(1)}, f32[520,128]{1,0:T(8,128)S(1)}, u32[]{:S(2)}, u32[]{:S(2)}) %collective-permute-start) | collective-permute-done | bytes 266272 | tf_op jit(solution)/shard_map/ppermute | solution.py:231
  10.0 0.0 copy-done.1
  10.1 13.7 %all_to_all.10.got_ref = f32[16,40,128]{2,1,0:T(8,128)S(1)} all-to-all(f32[16,40,128]{2,1,0:T(8,128)S(1)} %pad_maximum_fusion), channel_id=1, replica_groups=mesh['y'=4,'xh'=2,'z'=8,'xl'=2,'c'=2] {'y','xh','xl'}, dimensions={0} | all-to-all | bytes 655360 | tf_op jit(solution)/shard_map/all_to_all | solution.py:242
  23.8 5.7 %collective-permute-start.1 = (f32[48,128]{1,0:T(8,128)S(1)}, f32[48,128]{1,0:T(8,128)S(1)}, u32[]{:S(2)}, u32[]{:S(2)}) collective-permute-start(f32[48,128]{1,0:T(8,128)S(1)} %pad_maximum_fusion.3), channel_id=1, source_target_pairs={{0,28},{4,24},{8,20},{12,16},{16,12},{20,8},{24,4},{28,0},{1,29},{... | collective-permute-start | bytes 73736 | tf_op jit(solution)/shard_map/ppermute | solution.py:247
  29.5 1.2 %collective-permute-done.1 = f32[48,128]{1,0:T(8,128)S(1)} collective-permute-done((f32[48,128]{1,0:T(8,128)S(1)}, f32[48,128]{1,0:T(8,128)S(1)}, u32[]{:S(2)}, u32[]{:S(2)}) %collective-permute-start.1) | collective-permute-done | bytes 24608 | tf_op jit(solution)/shard_map/ppermute | solution.py:247
  30.7 1.7 %collective-permute-start.2 = (f32[64,128]{1,0:T(8,128)S(1)}, f32[64,128]{1,0:T(8,128)S(1)}, u32[]{:S(2)}, u32[]{:S(2)}) collective-permute-start(f32[64,128]{1,0:T(8,128)S(1)} %pad_maximum_fusion.2), channel_id=1, source_target_pairs={{0,4},{4,0},{8,12},{12,8},{16,20},{20,16},{24,28},{28,24},{1,5},{5... | collective-permute-start | bytes 98312 | tf_op jit(solution)/shard_map/ppermute | solution.py:247
  32.4 1.3 %collective-permute-done.2 = f32[64,128]{1,0:T(8,128)S(1)} collective-permute-done((f32[64,128]{1,0:T(8,128)S(1)}, f32[64,128]{1,0:T(8,128)S(1)}, u32[]{:S(2)}, u32[]{:S(2)}) %collective-permute-start.2) | collective-permute-done | bytes 32800 | tf_op jit(solution)/shard_map/ppermute | solution.py:247
  33.7 2.0 %collective-permute-start.3 = (f32[96,128]{1,0:T(8,128)S(1)}, f32[96,128]{1,0:T(8,128)S(1)}, u32[]{:S(2)}, u32[]{:S(2)}) collective-permute-start(f32[96,128]{1,0:T(8,128)S(1)} %pad_maximum_fusion.1.block_ref), channel_id=1, source_target_pairs={{0,8},{4,12},{8,0},{12,4},{16,24},{20,28},{24,16},{28,20},{1,9},{5... | collective-permute-start | bytes 147464 | tf_op jit(solution)/shard_map/ppermute | solution.py:247
  35.7 1.9 %collective-permute-done.3.peer_ref = f32[96,128]{1,0:T(8,128)S(1)} collective-permute-done((f32[96,128]{1,0:T(8,128)S(1)}, f32[96,128]{1,0:T(8,128)S(1)}, u32[]{:S(2)}, u32[]{:S(2)}) %collective-permute-start.3) | collective-permute-done | bytes 49184 | tf_op jit(solution)/shard_map/ppermute | solution.py:247
  37.7 2.0 %hals.1 = f32[16,32,128]{2,1,0:T(8,128)S(1)} custom-call(f32[96,128]{1,0:T(8,128)S(1)} %pad_maximum_fusion.1.block_ref, f32[96,128]{1,0:T(8,128)S(1)} %collective-permute-done.3.peer_ref, f32[16,40,128]{2,1,0:T(8,128)S(1)} %all_to_all.10.got_ref, f32[128,128]{1,0:T(8,128)S(1)} %get-tuple-element.8.gram_ref, f32[32,128]{1,0:T(8,128)S(1)} %get-tuple-element.9.old_ref), custom_call_target="tpu_custom_call" | custom-call | tf_op jit(solution)/shard_map/hals/pallas_call | solution.py:251
  39.7 10.3 %all_to_all.11 = f32[16,32,128]{2,1,0:T(8,128)S(1)} all-to-all(f32[16,32,128]{2,1,0:T(8,128)S(1)} %hals.1), channel_id=1, replica_groups=mesh['y'=4,'xh'=2,'z'=8,'xl'=2,'c'=2] {'y','xh','xl'}, dimensions={0} | all-to-all | bytes 524288 | tf_op jit(solution)/shard_map/all_to_all | solution.py:259
  50.0 5.7 %collective-permute-start.4 = (f32[512,128]{1,0:T(8,128)S(1)}, f32[512,128]{1,0:T(8,128)S(1)}, u32[]{:S(2)}, u32[]{:S(2)}) collective-permute-start(f32[512,128]{1,0:T(8,128)S(1)} %bitcast.4), channel_id=1, source_target_pairs={{0,1},{1,0},{2,3},{3,2},{4,5},{5,4},{6,7},{7,6},{8,9},{9,8},{10,11... | collective-permute-start | bytes 786440 | tf_op jit(solution)/shard_map/ppermute | solution.py:260
  55.7 0.3 half_gram.1.part_ref
  56.0 0.9 %collective-permute-done.4.other_ref = f32[512,128]{1,0:T(8,128)S(1)} collective-permute-done((f32[512,128]{1,0:T(8,128)S(1)}, f32[512,128]{1,0:T(8,128)S(1)}, u32[]{:S(2)}, u32[]{:S(2)}) %collective-permute-start.4) | collective-permute-done | bytes 262176 | tf_op jit(solution)/shard_map/ppermute | solution.py:260
  56.9 1.1 %finish.1 = (f32[1024,128]{1,0:T(8,128)}, f32[128,128]{1,0:T(8,128)}) custom-call(f32[512,128]{1,0:T(8,128)S(1)} %bitcast.6, f32[512,128]{1,0:T(8,128)S(1)} %collective-permute-done.4.other_ref, f32[128,128]{1,0:T(8,128)S(1)} %half_gram.1.part_ref), custom_call_target="tpu_custom_call" | custom-call | tf_op jit(solution)/shard_map/finish/pallas_call | solution.py:158
  (16 shorter events, 0.2 us)
Async XLA Ops:
  0.6 9.3 %copy-start.1 = (f32[4,128]{1,0:T(4,128)S(1)}, f32[4,128]{1,0:T(4,128)}, u32[]{:S(2)}) copy-start(f32[4,128]{1,0:T(4,128)} %three_hbm.1) | copy-start | bytes 6148
  0.6 8.1 %copy-start = (f32[8,128]{1,0:T(8,128)S(1)}, f32[8,128]{1,0:T(8,128)}, u32[]{:S(2)}) copy-start(f32[8,128]{1,0:T(8,128)} %two_hbm.1) | copy-start | bytes 12292
  5.5 4.5 %collective-permute-start = (f32[520,128]{1,0:T(8,128)S(1)}, f32[520,128]{1,0:T(8,128)S(1)}, u32[]{:S(2)}, u32[]{:S(2)}) collective-permute-start(f32[520,128]{1,0:T(8,128)S(1)} %get-tuple-element.7), channel_id=1, source_target_pairs={{0,1},{1,0},{2,3},{3,2},{4,5},{5,4},{6,7},{7,6},{8,9},{9,8},{10,11... | collective-permute-start | bytes 798728 | tf_op jit(solution)/shard_map/ppermute | solution.py:231
  23.8 6.9 %collective-permute-start.1 = (f32[48,128]{1,0:T(8,128)S(1)}, f32[48,128]{1,0:T(8,128)S(1)}, u32[]{:S(2)}, u32[]{:S(2)}) collective-permute-start(f32[48,128]{1,0:T(8,128)S(1)} %pad_maximum_fusion.3), channel_id=1, source_target_pairs={{0,28},{4,24},{8,20},{12,16},{16,12},{20,8},{24,4},{28,0},{1,29},{... | collective-permute-start | bytes 73736 | tf_op jit(solution)/shard_map/ppermute | solution.py:247
  30.7 3.0 %collective-permute-start.2 = (f32[64,128]{1,0:T(8,128)S(1)}, f32[64,128]{1,0:T(8,128)S(1)}, u32[]{:S(2)}, u32[]{:S(2)}) collective-permute-start(f32[64,128]{1,0:T(8,128)S(1)} %pad_maximum_fusion.2), channel_id=1, source_target_pairs={{0,4},{4,0},{8,12},{12,8},{16,20},{20,16},{24,28},{28,24},{1,5},{5... | collective-permute-start | bytes 98312 | tf_op jit(solution)/shard_map/ppermute | solution.py:247
  33.7 3.9 %collective-permute-start.3 = (f32[96,128]{1,0:T(8,128)S(1)}, f32[96,128]{1,0:T(8,128)S(1)}, u32[]{:S(2)}, u32[]{:S(2)}) collective-permute-start(f32[96,128]{1,0:T(8,128)S(1)} %pad_maximum_fusion.1.block_ref), channel_id=1, source_target_pairs={{0,8},{4,12},{8,0},{12,4},{16,24},{20,28},{24,16},{28,20},{1,9},{5... | collective-permute-start | bytes 147464 | tf_op jit(solution)/shard_map/ppermute | solution.py:247
  50.0 6.9 %collective-permute-start.4 = (f32[512,128]{1,0:T(8,128)S(1)}, f32[512,128]{1,0:T(8,128)S(1)}, u32[]{:S(2)}, u32[]{:S(2)}) collective-permute-start(f32[512,128]{1,0:T(8,128)S(1)} %bitcast.4), channel_id=1, source_target_pairs={{0,1},{1,0},{2,3},{3,2},{4,5},{5,4},{6,7},{7,6},{8,9},{9,8},{10,11... | collective-permute-start | bytes 786440 | tf_op jit(solution)/shard_map/ppermute | solution.py:260

commit v4 on v3

--- a/solution.py
+++ b/solution.py
@@ -7,7 +7,7 @@
 
 HIGHEST = lax.Precision.HIGHEST
 PLANE = ("y", "xh", "xl")
-Z_MASKS = (7, 1, 2)
+Z_MASKS = (1, 2, 7)
 IN_VMEM = pl.BlockSpec(memory_space=pltpu.VMEM)
 IN_PLACE = pl.BlockSpec(memory_space=pl.ANY)
 

time: 58.1 us -> 58.1 us (level)
  no operation moved by 1% of the time
where the time goes in v4:
time: 58.1 us; the launch traced here: 58 us
  blocking collectives  24 us (41%)
  starting transfers between devices  18.8 us (32%)
  Pallas kernels  8.18 us (14%)
  waiting for transfers between devices  6.03 us (10%)
  between operations  0.73 us (1%)
    all_to_all x1, blocking collectives, per_device(): got = lax.all_to_all(blocks, PLANE, 0, 0, tiled=True)  13.7 us
    all_to_all x1, blocking collectives, per_device(): lax.all_to_all(spread, PLANE, 0, 0, tiled=True).reshape(half, rank)  10.3 us
    ppermute x3, starting transfers between devices, per_device(): peer = lax.ppermute(block, 'z', [(i, i ^ mask) for i in range(depth)])  9.65 us
    ppermute x1, starting transfers between devices, per_device(): other_new = lax.ppermute(mine_new, 'c', swap)  5.89 us
    pallas_call x1, Pallas kernels, contract(): pl.pallas_call(contract_kernel, out_shape=(pltpu.VMEM((half + 2 * three.s...  4.84 us
    ppermute x3, waiting for transfers between devices, per_device(): peer = lax.ppermute(block, 'z', [(i, i ^ mask) for i in range(depth)])  4.01 us
    ppermute x1, starting transfers between devices, per_device(): other = lax.ppermute(send, 'c', swap)  3.28 us
    pallas_call x1, Pallas kernels, per_device(): pl.pallas_call(hals_kernel, out_shape=pltpu.VMEM((plane, rows, rank), jnp...  1.99 us
  transfers between devices with their start and end apart: 5, of which 5 were waited for; matrix products, arithmetic and copies ran while one was open for 0% of the time, Pallas kernels for 1%

profile of v4, /device:TPU:1, one launch (start us, length us, event | category | flops | bytes accessed | tf_op | source)
XLA Modules:
  0.0 58.0 jit_solution(8650205463649182670)
XLA Ops:
  0.6 0.0 copy-start.1
  0.6 0.0 copy-start
  0.7 4.8 %contract.1 = (f32[520,128]{1,0:T(8,128)S(1)}, f32[512,128]{1,0:T(8,128)S(1)}, f32[32,128]{1,0:T(8,128)S(1)}, f32[128,128]{1,0:T(8,128)S(1)}) custom-call(f32[2048,1024]{1,0:T(8,128)} %bitcast.7, f32[1024,128]{1,0:T(8,128)} %one_hbm.1, f32[8,128]{1,0:T(8,128)} %two_hbm.1, f32[4,128]{1,0:T(4,128)} %three_hbm.1, f32[64,128]{1,0:T(8,128)} %four_hbm.1), custom_call_target="tpu_custom_call" | custom-call | tf_op jit(solution)/shard_map/contract/pallas_call | solution.py:97
  5.5 3.3 %collective-permute-start = (f32[520,128]{1,0:T(8,128)S(1)}, f32[520,128]{1,0:T(8,128)S(1)}, u32[]{:S(2)}, u32[]{:S(2)}) collective-permute-start(f32[520,128]{1,0:T(8,128)S(1)} %get-tuple-element.7), channel_id=1, source_target_pairs={{0,1},{1,0},{2,3},{3,2},{4,5},{5,4},{6,7},{7,6},{8,9},{9,8},{10,11... | collective-permute-start | bytes 798728 | tf_op jit(solution)/shard_map/ppermute | solution.py:231
  8.8 0.0 copy-done
  8.8 1.2 %collective-permute-done = f32[520,128]{1,0:T(8,128)S(1)} collective-permute-done((f32[520,128]{1,0:T(8,128)S(1)}, f32[520,128]{1,0:T(8,128)S(1)}, u32[]{:S(2)}, u32[]{:S(2)}) %collective-permute-start) | collective-permute-done | bytes 266272 | tf_op jit(solution)/shard_map/ppermute | solution.py:231
  10.0 0.0 copy-done.1
  10.1 13.7 %all_to_all.10.got_ref = f32[16,40,128]{2,1,0:T(8,128)S(1)} all-to-all(f32[16,40,128]{2,1,0:T(8,128)S(1)} %pad_maximum_fusion), channel_id=1, replica_groups=mesh['y'=4,'xh'=2,'z'=8,'xl'=2,'c'=2] {'y','xh','xl'}, dimensions={0} | all-to-all | bytes 655360 | tf_op jit(solution)/shard_map/all_to_all | solution.py:242
  23.8 1.7 %collective-permute-start.1 = (f32[48,128]{1,0:T(8,128)S(1)}, f32[48,128]{1,0:T(8,128)S(1)}, u32[]{:S(2)}, u32[]{:S(2)}) collective-permute-start(f32[48,128]{1,0:T(8,128)S(1)} %pad_maximum_fusion.3), channel_id=1, source_target_pairs={{0,4},{4,0},{8,12},{12,8},{16,20},{20,16},{24,28},{28,24},{1,5},{5... | collective-permute-start | bytes 73736 | tf_op jit(solution)/shard_map/ppermute | solution.py:247
  25.5 1.2 %collective-permute-done.1 = f32[48,128]{1,0:T(8,128)S(1)} collective-permute-done((f32[48,128]{1,0:T(8,128)S(1)}, f32[48,128]{1,0:T(8,128)S(1)}, u32[]{:S(2)}, u32[]{:S(2)}) %collective-permute-start.1) | collective-permute-done | bytes 24608 | tf_op jit(solution)/shard_map/ppermute | solution.py:247
  26.8 3.1 %collective-permute-start.2 = (f32[64,128]{1,0:T(8,128)S(1)}, f32[64,128]{1,0:T(8,128)S(1)}, u32[]{:S(2)}, u32[]{:S(2)}) collective-permute-start(f32[64,128]{1,0:T(8,128)S(1)} %pad_maximum_fusion.2), channel_id=1, source_target_pairs={{0,8},{4,12},{8,0},{12,4},{16,24},{20,28},{24,16},{28,20},{1,9},{5... | collective-permute-start | bytes 98312 | tf_op jit(solution)/shard_map/ppermute | solution.py:247
  29.9 1.3 %collective-permute-done.2 = f32[64,128]{1,0:T(8,128)S(1)} collective-permute-done((f32[64,128]{1,0:T(8,128)S(1)}, f32[64,128]{1,0:T(8,128)S(1)}, u32[]{:S(2)}, u32[]{:S(2)}) %collective-permute-start.2) | collective-permute-done | bytes 32800 | tf_op jit(solution)/shard_map/ppermute | solution.py:247
  31.2 4.8 %collective-permute-start.3 = (f32[96,128]{1,0:T(8,128)S(1)}, f32[96,128]{1,0:T(8,128)S(1)}, u32[]{:S(2)}, u32[]{:S(2)}) collective-permute-start(f32[96,128]{1,0:T(8,128)S(1)} %pad_maximum_fusion.1.block_ref), channel_id=1, source_target_pairs={{0,28},{4,24},{8,20},{12,16},{16,12},{20,8},{24,4},{28,0},{1,29},{... | collective-permute-start | bytes 147464 | tf_op jit(solution)/shard_map/ppermute | solution.py:247
  36.0 1.5 %collective-permute-done.3.peer_ref = f32[96,128]{1,0:T(8,128)S(1)} collective-permute-done((f32[96,128]{1,0:T(8,128)S(1)}, f32[96,128]{1,0:T(8,128)S(1)}, u32[]{:S(2)}, u32[]{:S(2)}) %collective-permute-start.3) | collective-permute-done | bytes 49184 | tf_op jit(solution)/shard_map/ppermute | solution.py:247
  37.5 2.0 %hals.1 = f32[16,32,128]{2,1,0:T(8,128)S(1)} custom-call(f32[96,128]{1,0:T(8,128)S(1)} %pad_maximum_fusion.1.block_ref, f32[96,128]{1,0:T(8,128)S(1)} %collective-permute-done.3.peer_ref, f32[16,40,128]{2,1,0:T(8,128)S(1)} %all_to_all.10.got_ref, f32[128,128]{1,0:T(8,128)S(1)} %get-tuple-element.8.gram_ref, f32[32,128]{1,0:T(8,128)S(1)} %get-tuple-element.9.old_ref), custom_call_target="tpu_custom_call" | custom-call | tf_op jit(solution)/shard_map/hals/pallas_call | solution.py:251
  39.5 10.3 %all_to_all.11 = f32[16,32,128]{2,1,0:T(8,128)S(1)} all-to-all(f32[16,32,128]{2,1,0:T(8,128)S(1)} %hals.1), channel_id=1, replica_groups=mesh['y'=4,'xh'=2,'z'=8,'xl'=2,'c'=2] {'y','xh','xl'}, dimensions={0} | all-to-all | bytes 524288 | tf_op jit(solution)/shard_map/all_to_all | solution.py:259
  49.9 5.9 %collective-permute-start.4 = (f32[512,128]{1,0:T(8,128)S(1)}, f32[512,128]{1,0:T(8,128)S(1)}, u32[]{:S(2)}, u32[]{:S(2)}) collective-permute-start(f32[512,128]{1,0:T(8,128)S(1)} %bitcast.4), channel_id=1, source_target_pairs={{0,1},{1,0},{2,3},{3,2},{4,5},{5,4},{6,7},{7,6},{8,9},{9,8},{10,11... | collective-permute-start | bytes 786440 | tf_op jit(solution)/shard_map/ppermute | solution.py:260
  55.7 0.3 half_gram.1.part_ref
  56.0 0.9 %collective-permute-done.4.other_ref = f32[512,128]{1,0:T(8,128)S(1)} collective-permute-done((f32[512,128]{1,0:T(8,128)S(1)}, f32[512,128]{1,0:T(8,128)S(1)}, u32[]{:S(2)}, u32[]{:S(2)}) %collective-permute-start.4) | collective-permute-done | bytes 262176 | tf_op jit(solution)/shard_map/ppermute | solution.py:260
  56.9 1.1 %finish.1 = (f32[1024,128]{1,0:T(8,128)}, f32[128,128]{1,0:T(8,128)}) custom-call(f32[512,128]{1,0:T(8,128)S(1)} %bitcast.6, f32[512,128]{1,0:T(8,128)S(1)} %collective-permute-done.4.other_ref, f32[128,128]{1,0:T(8,128)S(1)} %half_gram.1.part_ref), custom_call_target="tpu_custom_call" | custom-call | tf_op jit(solution)/shard_map/finish/pallas_call | solution.py:158
  (16 shorter events, 0.2 us)
Async XLA Ops:
  0.6 9.3 %copy-start.1 = (f32[4,128]{1,0:T(4,128)S(1)}, f32[4,128]{1,0:T(4,128)}, u32[]{:S(2)}) copy-start(f32[4,128]{1,0:T(4,128)} %three_hbm.1) | copy-start | bytes 6148
  0.6 8.1 %copy-start = (f32[8,128]{1,0:T(8,128)S(1)}, f32[8,128]{1,0:T(8,128)}, u32[]{:S(2)}) copy-start(f32[8,128]{1,0:T(8,128)} %two_hbm.1) | copy-start | bytes 12292
  5.5 4.5 %collective-permute-start = (f32[520,128]{1,0:T(8,128)S(1)}, f32[520,128]{1,0:T(8,128)S(1)}, u32[]{:S(2)}, u32[]{:S(2)}) collective-permute-start(f32[520,128]{1,0:T(8,128)S(1)} %get-tuple-element.7), channel_id=1, source_target_pairs={{0,1},{1,0},{2,3},{3,2},{4,5},{5,4},{6,7},{7,6},{8,9},{9,8},{10,11... | collective-permute-start | bytes 798728 | tf_op jit(solution)/shard_map/ppermute | solution.py:231
  23.8 2.9 %collective-permute-start.1 = (f32[48,128]{1,0:T(8,128)S(1)}, f32[48,128]{1,0:T(8,128)S(1)}, u32[]{:S(2)}, u32[]{:S(2)}) collective-permute-start(f32[48,128]{1,0:T(8,128)S(1)} %pad_maximum_fusion.3), channel_id=1, source_target_pairs={{0,4},{4,0},{8,12},{12,8},{16,20},{20,16},{24,28},{28,24},{1,5},{5... | collective-permute-start | bytes 73736 | tf_op jit(solution)/shard_map/ppermute | solution.py:247
  26.8 4.4 %collective-permute-start.2 = (f32[64,128]{1,0:T(8,128)S(1)}, f32[64,128]{1,0:T(8,128)S(1)}, u32[]{:S(2)}, u32[]{:S(2)}) collective-permute-start(f32[64,128]{1,0:T(8,128)S(1)} %pad_maximum_fusion.2), channel_id=1, source_target_pairs={{0,8},{4,12},{8,0},{12,4},{16,24},{20,28},{24,16},{28,20},{1,9},{5... | collective-permute-start | bytes 98312 | tf_op jit(solution)/shard_map/ppermute | solution.py:247
  31.2 6.3 %collective-permute-start.3 = (f32[96,128]{1,0:T(8,128)S(1)}, f32[96,128]{1,0:T(8,128)S(1)}, u32[]{:S(2)}, u32[]{:S(2)}) collective-permute-start(f32[96,128]{1,0:T(8,128)S(1)} %pad_maximum_fusion.1.block_ref), channel_id=1, source_target_pairs={{0,28},{4,24},{8,20},{12,16},{16,12},{20,8},{24,4},{28,0},{1,29},{... | collective-permute-start | bytes 147464 | tf_op jit(solution)/shard_map/ppermute | solution.py:247
  49.9 7.1 %collective-permute-start.4 = (f32[512,128]{1,0:T(8,128)S(1)}, f32[512,128]{1,0:T(8,128)S(1)}, u32[]{:S(2)}, u32[]{:S(2)}) collective-permute-start(f32[512,128]{1,0:T(8,128)S(1)} %bitcast.4), channel_id=1, source_target_pairs={{0,1},{1,0},{2,3},{3,2},{4,5},{5,4},{6,7},{7,6},{8,9},{9,8},{10,11... | collective-permute-start | bytes 786440 | tf_op jit(solution)/shard_map/ppermute | solution.py:260
